TPU v7x, 32 devices: a whole 2x2x4 slice. The times are simulated.
32 devices in a mesh: batch: 4 (over y, x), rows: 8 (over z, core).
Axes of the slice: x: 2, y: 2, z: 4, core: 2. Of those that a mesh axis runs over, the one named last changes fastest.
Arguments:
- features: bfloat16 [256, 8, 16, 2048], P('batch', 'rows'), may hold values from -6 to 6
- w_reduce: bfloat16 [2048, 512], P('rows'), may hold values from -0.125 to 0.125
- w_spatial: bfloat16 [4608, 512], P('rows'), may hold values from -0.09375 to 0.09375
- w_expand: bfloat16 [512, 2048], P('rows'), may hold values from -0.25 to 0.25
- query_weight: bfloat16 [2048, 512], P('rows'), may hold values from -0.125 to 0.125
- w_key: bfloat16 [2048, 512], P('rows'), may hold values from -0.125 to 0.125
- w_value: bfloat16 [2048, 512], P('rows'), may hold values from -0.125 to 0.125
- w_out: bfloat16 [512, 2048], P('rows'), may hold values from -0.5 to 0.5
- w_head: bfloat16 [4096, 80], P('rows'), may hold values from -0.09375 to 0.09375
- gain_a: float32 [512], replicated, may hold values from 0.1 to 1.9
- bias_a: float32 [512], replicated, may hold values from -0.5 to 0.5
- gain_b: float32 [512], replicated, may hold values from 0.1 to 1.9
- bias_b: float32 [512], replicated, may hold values from -0.5 to 0.5
- gain_c: float32 [2048], replicated, may hold values from 0.1 to 1.9
- bias_c: float32 [2048], replicated, may hold values from -0.5 to 0.5
- ln_gain: float32 [512], replicated, may hold values from 0.1 to 1.9
- ln_bias: float32 [512], replicated, may hold values from -0.5 to 0.5
- head_bias: float32 [80], replicated, may hold values from -1 to 1
- bank: bfloat16 [320, 2048], P(('batch', 'rows')), may hold values from -6 to 6
- piece_box: int32 [256, 8], P(('batch', 'rows')), may hold values from 0 to 127
- piece_clip: int32 [256, 8], P(('batch', 'rows')), may hold values from 0 to 63
- send_count: int32 [256], P(('batch', 'rows')), may hold values from 0 to 8, as said below
- sample_pos: int32 [256, 224], P(('batch', 'rows')), may hold values from 0 to 15
- sample_weight: float32 [256, 224], P(('batch', 'rows')), may hold values from 0.01 to 0.06
- win_start: int32 [4096], P(('batch', 'rows')), may hold values from 0 to 60, as said below
- win_len: int32 [4096], P(('batch', 'rows')), may hold values from 20 to 40, as said below
- prob_cotangent: float32 [4096, 80], P(('batch', 'rows')), may hold values from -6 to 6
Outputs:
- probs: float32 [4096, 80], P(('batch', 'rows'))
- features_grad: bfloat16 [256, 8, 16, 2048], P('batch', 'rows')
- w_reduce_grad: float32 [2048, 512], P('rows', 'batch')
- w_spatial_grad: float32 [4608, 512], P('rows', 'batch')
- w_expand_grad: float32 [512, 2048], P('rows', 'batch')
- w_query_grad: float32 [2048, 512], P('rows', 'batch')
- w_key_grad: float32 [2048, 512], P('rows', 'batch')
- w_value_grad: float32 [2048, 512], P('rows', 'batch')
- w_out_grad: float32 [512, 2048], P('rows', 'batch')
- w_head_grad: float32 [4096, 80], P('rows', 'batch')
- gain_a_grad: float32 [512], replicated
- bias_a_grad: float32 [512], replicated
- gain_b_grad: float32 [512], replicated
- bias_b_grad: float32 [512], replicated
- gain_c_grad: float32 [2048], replicated
- bias_c_grad: float32 [2048], replicated
- ln_gain_grad: float32 [512], replicated
- ln_bias_grad: float32 [512], replicated
- classifier_bias_gradient: float32 [80], replicated
Inputs may be any that keep to these rules, and one draw needn't show every extreme that they name: `send_count`: at most 8 live slots from one device to one owner; some device sends exactly 8 to some owner in every draw. `win_len`: every window holds 20 to 40 entries, some box's exactly 40. win_start + win_len <= 80.
All inputs are finite; a program needn't handle non-finite values.
Results may differ from a plain program's by a relative error of at most 0.024.
Values may be sent and summed in bfloat16 or wider, within the bound.
A program may use at most 256 MiB of HBM per device.

v0:
```python
import jax
import jax.numpy as jnp
from jax import lax
from jax.sharding import PartitionSpec as P


def padded(cells, sides, width):
    for axis, dim in sides:
        count = lax.axis_size(axis)
        ends = count - 1
        head = lax.slice_in_dim(cells, 0, width, axis=dim)
        tail = lax.slice_in_dim(cells, cells.shape[dim] - width, cells.shape[dim], axis=dim)
        cells = jnp.concatenate(
            [
                lax.ppermute(tail, axis, [(i, (i + 1) % count) for i in range(ends)]),
                cells,
                lax.ppermute(head, axis, [((i + 1) % count, i) for i in range(ends)]),
            ],
            axis=dim,
        )
    return cells


def split_up(value, dim, peers):
    shape = value.shape
    parts = value.reshape(*shape[:dim], peers, shape[dim] // peers, *shape[dim + 1 :])
    return jnp.moveaxis(parts, dim, 0)


def sum_at_owner(value, axis, dim):
    peers = lax.axis_size(axis)
    parts = lax.all_to_all(split_up(value, dim, peers), axis, 0, 0, tiled=True)
    return jnp.sum(parts.astype(jnp.float32), axis=0)


def side_by_side(arrays, axis, dim, along):
    ends, at = ([], 0)
    for a in arrays[:-1]:
        at += a.shape[along]
        ends.append(at)
    both = jnp.concatenate(arrays, axis=along)
    return tuple(jnp.split(sum_at_owner(both, axis, dim), ends, axis=along))


def tdot(left, right):
    return lax.dot_general(
        left, right, (((0,), (0,)), ((), ())), preferred_element_type=jnp.float32
    )


def ndot(left, right):
    return lax.dot_general(
        left, right, (((1,), (1,)), ((), ())), preferred_element_type=jnp.float32
    )


def silu_slope(value):
    sig = jax.nn.sigmoid(value)
    return sig * (1.0 + value * (1.0 - sig))


def normalize(field, total_count):
    sums, squares = lax.psum((jnp.sum(field, 0), jnp.sum(field * field, 0)), ("batch", "rows"))
    centre_value = sums / total_count
    inverse = lax.rsqrt(squares / total_count - centre_value * centre_value + 1e-05)
    return ((field - centre_value) * inverse, inverse)


def segment_totals(grad, normed):
    return lax.psum((jnp.sum(grad, 0), jnp.sum(grad * normed, 0)), ("batch", "rows"))


def norm_back(grad, normed, inverse, gain, shift_sum, gain_total_grad, total_count):
    return (
        gain * inverse * (grad - shift_sum / total_count - normed * gain_total_grad / total_count)
    )


def on_device(
    features,
    w_reduce,
    w_spatial,
    w_expand,
    query_weight,
    w_key,
    w_value,
    w_out,
    w_head,
    gain_a,
    bias_a,
    gain_b,
    bias_b,
    gain_c,
    bias_c,
    ln_gain,
    ln_bias,
    head_bias,
    bank,
    piece_box,
    piece_clip,
    send_count,
    sample_pos,
    sample_weight,
    win_start,
    win_len,
    prob_cotangent,
):
    owners = lax.axis_size("rows")
    clip_dev, row_dev, col_count, d_in = features.shape
    cell_count = clip_dev * row_dev * col_count
    total_count = cell_count * owners * lax.axis_size("batch")
    w_a, w_b, w_c, w_q, w_k, w_v, w_o, w_h = (
        lax.all_gather(w_reduce, "rows", axis=0, tiled=True),
        lax.all_gather(w_spatial, "rows", axis=0, tiled=True),
        lax.all_gather(w_expand, "rows", axis=0, tiled=True),
        lax.all_gather(query_weight, "rows", axis=0, tiled=True),
        lax.all_gather(w_key, "rows", axis=0, tiled=True),
        lax.all_gather(w_value, "rows", axis=0, tiled=True),
        lax.all_gather(w_out, "rows", axis=0, tiled=True),
        lax.all_gather(w_head, "rows", axis=0, tiled=True),
    )
    d_mid = w_a.shape[1]
    flat_x = features.reshape(cell_count, d_in)
    pre_a = jnp.dot(flat_x, w_a, preferred_element_type=jnp.float32)
    hat_a, inverse_a = normalize(pre_a, total_count)
    act_a = gain_a * hat_a + bias_a
    low_a = jax.nn.silu(act_a).astype(jnp.bfloat16)
    halo_a = padded(low_a.reshape(clip_dev, row_dev, col_count, d_mid), (("rows", 1),), 1)
    halo_a = jnp.pad(halo_a, ((0, 0), (0, 0), (1, 1), (0, 0)))
    window_a = jnp.concatenate(
        [
            halo_a[:, row_step : row_step + row_dev, col_step : col_step + col_count]
            for row_step in range(3)
            for col_step in range(3)
        ],
        axis=3,
    ).reshape(cell_count, 9 * d_mid)
    pre_b = jnp.dot(window_a, w_b, preferred_element_type=jnp.float32)
    hat_b, inverse_b = normalize(pre_b, total_count)
    act_b = gain_b * hat_b + bias_b
    low_b = jax.nn.silu(act_b).astype(jnp.bfloat16)
    pre_c = jnp.dot(low_b, w_c, preferred_element_type=jnp.float32)
    hat_c, inverse_c = normalize(pre_c, total_count)
    pre_out = gain_c * hat_c + bias_c + flat_x.astype(jnp.float32)
    fmap = jax.nn.silu(pre_out).astype(jnp.bfloat16)
    capacity = piece_box.shape[1]
    samples = sample_pos.shape[1] // capacity
    slot_count = owners * capacity
    sample_cells = (
        piece_clip[:, :, None] * (row_dev * col_count)
        + sample_pos.reshape(owners, capacity, samples)
    ).reshape(slot_count, samples)
    is_live = (jnp.arange(capacity)[None, :] < send_count[:, None]).reshape(slot_count)
    slot_weights = sample_weight.reshape(slot_count, samples) * is_live[:, None].astype(jnp.float32)
    cell_ids = jnp.arange(cell_count)[None, :]
    interp_sum = jnp.zeros((slot_count, cell_count), jnp.float32)
    for sample_index in range(samples):
        interp_sum = interp_sum + jnp.where(
            sample_cells[:, sample_index, None] == cell_ids,
            slot_weights[:, sample_index, None],
            0.0,
        )
    interpolated_value = interp_sum.astype(jnp.bfloat16)
    region_parts = (
        jnp.dot(interpolated_value, fmap, preferred_element_type=jnp.float32)
        .astype(jnp.bfloat16)
        .reshape(owners, capacity, d_in)
    )
    arrived, arrived_box = (
        lax.all_to_all(region_parts, "rows", split_axis=0, concat_axis=0, tiled=True),
        lax.all_to_all(piece_box, "rows", split_axis=0, concat_axis=0, tiled=True),
    )
    box_dev = win_start.shape[0]
    flat_box = arrived_box.reshape(slot_count)
    owner_hits = (flat_box[None, :] == jnp.arange(box_dev)[:, None]).astype(jnp.bfloat16)
    pooled = jnp.dot(
        owner_hits, arrived.reshape(slot_count, d_in), preferred_element_type=jnp.float32
    )
    pooled_low = pooled.astype(jnp.bfloat16)
    keys_own = jnp.dot(bank, w_k, preferred_element_type=jnp.float32).astype(jnp.bfloat16)
    values_own = jnp.dot(bank, w_v, preferred_element_type=jnp.float32).astype(jnp.bfloat16)
    key_rows, value_rows = (
        lax.all_gather(keys_own, "rows", axis=0, tiled=True),
        lax.all_gather(values_own, "rows", axis=0, tiled=True),
    )
    bank_length = key_rows.shape[0]
    queries = jnp.dot(pooled_low, w_q, preferred_element_type=jnp.float32).astype(jnp.bfloat16)
    score_scale = d_mid ** (-0.5)
    scores = ndot(queries, key_rows) * score_scale
    positions = jnp.arange(bank_length)[None, :]
    window_mask = (positions >= win_start[:, None]) & (positions < (win_start + win_len)[:, None])
    attend = jax.nn.softmax(jnp.where(window_mask, scores, -1e30), axis=-1)
    attend_low = attend.astype(jnp.bfloat16)
    mixture = jnp.dot(attend_low, value_rows, preferred_element_type=jnp.float32)
    centred = mixture - jnp.mean(mixture, axis=-1, keepdims=True)
    inverse_z = lax.rsqrt(jnp.mean(centred * centred, axis=-1, keepdims=True) + 1e-05)
    hat_z = centred * inverse_z
    pre_ln = ln_gain * hat_z + ln_bias
    low_r = jax.nn.silu(pre_ln).astype(jnp.bfloat16)
    branch = jnp.dot(low_r, w_o, preferred_element_type=jnp.float32)
    joined = jnp.concatenate([pooled, pooled + branch], axis=1).astype(jnp.bfloat16)
    logits = jnp.dot(joined, w_h, preferred_element_type=jnp.float32) + head_bias
    likely = jax.nn.sigmoid(logits)
    d_logit = (prob_cotangent * (likely * (1.0 - likely))).astype(jnp.bfloat16)
    grad_head_bias = jnp.sum(d_logit.astype(jnp.float32), 0)
    grad_wh = tdot(joined, d_logit)
    d_joined = ndot(d_logit, w_h)
    d_pooled = d_joined[:, :d_in] + d_joined[:, d_in:]
    d_branch = d_joined[:, d_in:].astype(jnp.bfloat16)
    grad_wo = tdot(low_r, d_branch)
    d_ln = ndot(d_branch, w_o) * silu_slope(pre_ln)
    grad_ln_gain = jnp.sum(d_ln * hat_z, 0)
    grad_ln_bias = jnp.sum(d_ln, 0)
    d_hat = d_ln * ln_gain
    d_mixture = (
        inverse_z
        * (
            d_hat
            - jnp.mean(d_hat, axis=-1, keepdims=True)
            - hat_z * jnp.mean(d_hat * hat_z, axis=-1, keepdims=True)
        )
    ).astype(jnp.bfloat16)
    d_attend = ndot(d_mixture, value_rows)
    d_values = tdot(attend_low, d_mixture)
    d_scores = (attend * (d_attend - jnp.sum(d_attend * attend, axis=-1, keepdims=True))).astype(
        jnp.bfloat16
    )
    d_queries = (
        jnp.dot(d_scores, key_rows, preferred_element_type=jnp.float32) * score_scale
    ).astype(jnp.bfloat16)
    d_keys = tdot(d_scores, queries) * score_scale
    grad_wq = tdot(pooled_low, d_queries)
    d_pooled = d_pooled + ndot(d_queries, w_q)
    key_sum, value_sum = side_by_side(
        (d_keys.astype(jnp.bfloat16), d_values.astype(jnp.bfloat16)), "rows", 0, 1
    )
    grad_wk = tdot(bank, key_sum.astype(jnp.bfloat16))
    grad_wv = tdot(bank, value_sum.astype(jnp.bfloat16))
    back_pieces = jnp.take(d_pooled.astype(jnp.bfloat16), flat_box, axis=0).reshape(
        owners, capacity, d_in
    )
    returned = lax.all_to_all(back_pieces, "rows", split_axis=0, concat_axis=0, tiled=True)
    d_fmap = tdot(interpolated_value, returned.reshape(slot_count, d_in))
    d_pre = d_fmap * silu_slope(pre_out)
    head_sums = lax.psum(
        (jnp.sum(d_pre, 0), jnp.sum(d_pre * hat_c, 0), grad_ln_gain, grad_ln_bias, grad_head_bias),
        ("batch", "rows"),
    )
    d_c = norm_back(
        d_pre, hat_c, inverse_c, gain_c, head_sums[0], head_sums[1], total_count
    ).astype(jnp.bfloat16)
    grad_wc = tdot(low_b, d_c)
    d_act_b = ndot(d_c, w_c) * silu_slope(act_b)
    shift_b_sum, gain_b_sum = segment_totals(d_act_b, hat_b)
    d_b = norm_back(d_act_b, hat_b, inverse_b, gain_b, shift_b_sum, gain_b_sum, total_count).astype(
        jnp.bfloat16
    )
    grad_wb = tdot(window_a, d_b)
    halo_d = padded(d_b.reshape(clip_dev, row_dev, col_count, d_mid), (("rows", 1),), 1)
    halo_d = jnp.pad(halo_d, ((0, 0), (0, 0), (1, 1), (0, 0)))
    window_d = jnp.concatenate(
        [
            halo_d[
                :, 2 - row_step : 2 - row_step + row_dev, 2 - col_step : 2 - col_step + col_count
            ]
            for row_step in range(3)
            for col_step in range(3)
        ],
        axis=3,
    ).reshape(cell_count, 9 * d_mid)
    flipped = w_b.reshape(9, d_mid, d_mid).transpose(0, 2, 1).reshape(9 * d_mid, d_mid)
    d_act_a = jnp.dot(window_d, flipped, preferred_element_type=jnp.float32) * silu_slope(act_a)
    shift_a_sum, gain_a_sum = segment_totals(d_act_a, hat_a)
    d_a = norm_back(d_act_a, hat_a, inverse_a, gain_a, shift_a_sum, gain_a_sum, total_count).astype(
        jnp.bfloat16
    )
    grad_wa = tdot(flat_x, d_a)
    grad_input = (ndot(d_a, w_a) + d_pre).astype(jnp.bfloat16).reshape(features.shape)
    partial_sums = (
        lax.psum_scatter(grad_wa, "rows", scatter_dimension=0, tiled=True),
        lax.psum_scatter(grad_wb, "rows", scatter_dimension=0, tiled=True),
        lax.psum_scatter(grad_wc, "rows", scatter_dimension=0, tiled=True),
        lax.psum_scatter(grad_wq, "rows", scatter_dimension=0, tiled=True),
        lax.psum_scatter(grad_wk, "rows", scatter_dimension=0, tiled=True),
        lax.psum_scatter(grad_wv, "rows", scatter_dimension=0, tiled=True),
        lax.psum_scatter(grad_wo, "rows", scatter_dimension=0, tiled=True),
        lax.psum_scatter(grad_wh, "rows", scatter_dimension=0, tiled=True),
    )
    finished = (
        lax.psum_scatter(
            partial_sums[0].astype(jnp.bfloat16), "batch", scatter_dimension=1, tiled=True
        ).astype(jnp.float32),
        lax.psum_scatter(
            partial_sums[1].astype(jnp.bfloat16), "batch", scatter_dimension=1, tiled=True
        ).astype(jnp.float32),
        lax.psum_scatter(
            partial_sums[2].astype(jnp.bfloat16), "batch", scatter_dimension=1, tiled=True
        ).astype(jnp.float32),
        lax.psum_scatter(
            partial_sums[3].astype(jnp.bfloat16), "batch", scatter_dimension=1, tiled=True
        ).astype(jnp.float32),
        lax.psum_scatter(
            partial_sums[4].astype(jnp.bfloat16), "batch", scatter_dimension=1, tiled=True
        ).astype(jnp.float32),
        lax.psum_scatter(
            partial_sums[5].astype(jnp.bfloat16), "batch", scatter_dimension=1, tiled=True
        ).astype(jnp.float32),
        lax.psum_scatter(
            partial_sums[6].astype(jnp.bfloat16), "batch", scatter_dimension=1, tiled=True
        ).astype(jnp.float32),
        lax.psum_scatter(
            partial_sums[7].astype(jnp.bfloat16), "batch", scatter_dimension=1, tiled=True
        ).astype(jnp.float32),
    )
    return (
        likely,
        grad_input,
        finished[0],
        finished[1],
        finished[2],
        finished[3],
        finished[4],
        finished[5],
        finished[6],
        finished[7],
        gain_a_sum,
        shift_a_sum,
        gain_b_sum,
        shift_b_sum,
        head_sums[1],
        head_sums[0],
        head_sums[2],
        head_sums[3],
        head_sums[4],
    )


def solution(mesh):
    return jax.shard_map(
        on_device,
        mesh=mesh,
        in_specs=(
            P("batch", "rows", None, None),
            P("rows", None),
            P("rows", None),
            P("rows", None),
            P("rows", None),
            P("rows", None),
            P("rows", None),
            P("rows", None),
            P("rows", None),
            P(),
            P(),
            P(),
            P(),
            P(),
            P(),
            P(),
            P(),
            P(),
            P(("batch", "rows"), None),
            P(("batch", "rows"), None),
            P(("batch", "rows"), None),
            P(("batch", "rows")),
            P(("batch", "rows"), None),
            P(("batch", "rows"), None),
            P(("batch", "rows")),
            P(("batch", "rows")),
            P(("batch", "rows"), None),
        ),
        out_specs=(
            P(("batch", "rows"), None),
            P("batch", "rows", None, None),
            P("rows", "batch"),
            P("rows", "batch"),
            P("rows", "batch"),
            P("rows", "batch"),
            P("rows", "batch"),
            P("rows", "batch"),
            P("rows", "batch"),
            P("rows", "batch"),
            P(),
            P(),
            P(),
            P(),
            P(),
            P(),
            P(),
            P(),
            P(),
        ),
        check_vma=False,
    )
```

profile of v0, /device:TPU:0, one launch (start us, length us, event | category | flops | bytes accessed | tf_op | source)
XLA Modules:
  0.0 1011.4 jit_solution(11663919438469440399)
XLA Ops:
  19.9 21.7 %all-gather.10.cloned.1.call-done = bf16[2048,512]{1,0:T(8,128)(2,1)} async-done(((bf16[256,512]{1,0:T(8,128)(2,1)}), bf16[2048,512]{1,0:T(8,128)(2,1)}) %all-gather.10.cloned.1.call-update) | async-done | bytes 2097168 | tf_op jit(solution)/shard_map/all_gather | solution.py:113
  46.9 42.2 %all-reduce.8 = (f32[512]{0:T(512)S(1)}, f32[512]{0:T(512)S(1)}) all-reduce(f32[512]{0:T(512)S(1)} %get-tuple-element.106, f32[512]{0:T(512)S(1)} %get-tuple-element.105), channel_id=1, replica_groups=mesh['batch'=4,'rows'=8] {'batch','rows'}, use_global_device_ids=true, to_apply=%region_3.0 | all-reduce | flops 1024 | bytes 8192 | tf_op jit(solution)/shard_map/psum | solution.py:63
  97.0 39.7 %all_gather.39 = bf16[4096,80]{0,1:T(8,128)(2,1)} all-gather(bf16[512,80]{0,1:T(8,128)(2,1)S(1)} %copy-done.8), channel_id=1, replica_groups=mesh['batch'=4,'rows'=8] {'rows'}, dimensions={0}, use_global_device_ids=true | all-gather | bytes 737280 | tf_op jit(solution)/shard_map/all_gather | solution.py:120
  157.1 10.1 %fusion.48 = (f32[512]{0:T(512)S(1)}, f32[512]{0:T(512)S(1)}, f32[1024,512]{1,0:T(8,128)}) fusion(bf16[1024,4608]{1,0:T(8,128)(2,1)} %constant_dynamic-update-slice_fusion, bf16[4608,512]{1,0:T(8,128)(2,1)} %all-gather.12.cloned.1.call-done), kind=kOutput, calls=%fused_computation.239 | convolution fusion | flops 4833410048 | bytes 16257024 | tf_op jit(solution)/shard_map/dot_general | solution.py:138
  167.2 41.5 %all-reduce.7 = (f32[512]{0:T(512)S(1)}, f32[512]{0:T(512)S(1)}) all-reduce(f32[512]{0:T(512)S(1)} %get-tuple-element.104, f32[512]{0:T(512)S(1)} %get-tuple-element.103), channel_id=1, replica_groups=mesh['batch'=4,'rows'=8] {'batch','rows'}, use_global_device_ids=true, to_apply=%region_7.8 | all-reduce | flops 1024 | bytes 8192 | tf_op jit(solution)/shard_map/psum | solution.py:63
  208.9 8.2 fusion.45
  217.0 42.3 %all-reduce.6 = (f32[2048]{0:T(1024)S(1)}, f32[2048]{0:T(1024)S(1)}) all-reduce(f32[2048]{0:T(1024)S(1)} %get-tuple-element.98, f32[2048]{0:T(1024)S(1)} %get-tuple-element.97), channel_id=1, replica_groups=mesh['batch'=4,'rows'=8] {'batch','rows'}, use_global_device_ids=true, to_apply=%region_11.12 | all-reduce | flops 4096 | bytes 32768 | tf_op jit(solution)/shard_map/psum | solution.py:63
  259.8 10.3 %fusion.6 = bf16[8,8,2048]{2,1,0:T(8,128)(2,1)} fusion(bf16[1024,2048]{1,0:T(8,128)(2,1)} %bitcast.110, f32[2048]{0:T(1024)S(1)} %copy-done.116, f32[2048]{0:T(1024)S(1)} %get-tuple-element.197, f32[1024,2048]{1,0:T(8,128)} %get-tuple-element.207, f32[2048]{0:T(1024)S(1)} %get-tuple-element.198, f32[2048]{0:T(1024)S(1)} %copy-done.20, ...), kind=kOutput, calls=%fused_computation.27 | convolution fusion | flops 297140224 | bytes 12892160 | tf_op jit(solution)/shard_map/dot_general | solution.py:165
  275.5 15.3 %all-gather = bf16[8,10,512]{2,1,0:T(8,128)(2,1)S(1)} all-gather(bf16[1,10,512]{2,1,0:T(8,128)(2,1)S(1)} %fusion.14), channel_id=1, replica_groups=mesh['batch'=4,'rows'=8] {'rows'}, dimensions={0}, use_global_device_ids=true | all-gather | bytes 92160 | tf_op jit(solution)/shard_map/all_gather | solution.py:183
  292.9 14.4 %all-gather.1 = bf16[8,10,512]{2,1,0:T(8,128)(2,1)S(1)} all-gather(bf16[1,10,512]{2,1,0:T(8,128)(2,1)S(1)} %fusion.15), channel_id=1, replica_groups=mesh['batch'=4,'rows'=8] {'rows'}, dimensions={0}, use_global_device_ids=true | all-gather | bytes 92160 | tf_op jit(solution)/shard_map/all_gather | solution.py:184
  332.2 16.3 %all_to_all.24 = bf16[8,10,1024]{2,1,0:T(8,128)(2,1)S(1)} all-to-all(bf16[8,10,1024]{2,1,0:T(8,128)(2,1)S(1)} %reshape.231), channel_id=1, replica_groups=mesh['batch'=4,'rows'=8] {'rows'}, dimensions={0} | all-to-all | bytes 327680 | tf_op jit(solution)/shard_map/all_to_all | solution.py:32
  358.5 17.0 %all_to_all.25 = bf16[8,8,2048]{2,1,0:T(8,128)(2,1)S(1)} all-to-all(bf16[8,8,2048]{2,1,0:T(8,128)(2,1)S(1)} %bitcast_select_fusion), channel_id=1, replica_groups=mesh['batch'=4,'rows'=8] {'rows'}, dimensions={0} | all-to-all | bytes 524288 | tf_op jit(solution)/shard_map/all_to_all | solution.py:242
  375.9 14.8 %fusion.44 = (f32[2048]{0:T(1024)S(1)}, f32[2048]{0:T(1024)S(1)}, f32[1024,2048]{1,0:T(8,128)}) fusion(f32[2048]{0:T(1024)S(1)} %get-tuple-element.197, f32[1024,2048]{1,0:T(8,128)} %get-tuple-element.207, f32[2048]{0:T(1024)S(1)} %get-tuple-element.198, bf16[1024,2048]{1,0:T(8,128)(2,1)} %bitcast.111, f32[2048]{0:T(1024)} %param.41, ...), kind=kOutput, calls=%fused_computation.235 | convolution fusion | flops 309587968 | bytes 21297152 | tf_op jit(solution)/shard_map/dot_general | solution.py:46
  390.7 38.9 %all-reduce.5 = (f32[2048]{0:T(1024)S(1)}, f32[2048]{0:T(1024)S(1)}) all-reduce(f32[2048]{0:T(1024)S(1)} %get-tuple-element.96, f32[2048]{0:T(1024)S(1)} %get-tuple-element.95), channel_id=1, replica_groups=mesh['batch'=4,'rows'=8] {'batch','rows'}, use_global_device_ids=true, to_apply=%region_22.23 | all-reduce | flops 4096 | bytes 32768 | tf_op jit(solution)/shard_map/psum | solution.py:245
  429.7 7.4 multiply_convert_fusion
  444.0 8.1 fusion.47
  452.1 42.8 %all-reduce.4 = (f32[512]{0:T(512)S(1)}, f32[512]{0:T(512)S(1)}) all-reduce(f32[512]{0:T(512)S(1)} %get-tuple-element.102, f32[512]{0:T(512)S(1)} %get-tuple-element.101), channel_id=1, replica_groups=mesh['batch'=4,'rows'=8] {'batch','rows'}, use_global_device_ids=true, to_apply=%region_26.27 | all-reduce | flops 1024 | bytes 8192 | tf_op jit(solution)/shard_map/psum | solution.py:70
  518.0 7.1 fusion.46
  525.2 53.3 %all-reduce.3 = (f32[512]{0:T(512)S(1)}, f32[512]{0:T(512)S(1)}, f32[512]{0:T(512)}, f32[512]{0:T(512)}, f32[80]{0:T(128)}) all-reduce(f32[512]{0:T(512)S(1)} %get-tuple-element.100, f32[512]{0:T(512)S(1)} %get-tuple-element.99, f32[512]{0:T(512)S(1)} %copy-done.28, ...), channel_id=1, replica_groups=mesh['batch'=4,'rows'=8] {'batch','rows'}, use_global_device_ids=true, to_apply=%region_30.31 | all-reduce | flops 2128 | bytes 17024 | tf_op jit(solution)/shard_map/psum | solution.py:70
  586.3 11.4 %fusion.57 = f32[4608,512]{1,0:T(8,128)} fusion(bf16[1024,4608]{1,0:T(8,128)(2,1)} %constant_dynamic-update-slice_fusion, bf16[1024,512]{1,0:T(8,128)(2,1)S(1)} %multiply_convert_fusion.8), kind=kOutput, calls=%fused_computation.247 | convolution fusion | flops 4831838208 | bytes 19922944 | tf_op jit(solution)/shard_map/dot_general | solution.py:46
  607.2 10.4 %reduce-scatter.26.cloned.1.call-done = f32[64,2048]{1,0:T(8,128)} async-done(((f32[512,2048]{1,0:T(8,128)}), f32[64,2048]{1,0:T(8,128)}) %reduce-scatter.26.cloned.1.call-update) | async-done | bytes 524304 | tf_op jit(solution)/shard_map/reduce_scatter | solution.py:282
  619.5 49.1 %reduce-scatter.20.cloned.1.call-done = f32[256,512]{0,1:T(8,128)} async-done(((f32[2048,512]{0,1:T(8,128)}), f32[256,512]{0,1:T(8,128)}) %reduce-scatter.20.cloned.1.call-update) | async-done | bytes 524304 | tf_op jit(solution)/shard_map/reduce_scatter | solution.py:280
  670.4 98.0 %reduce-scatter.24.cloned.1.call-done = f32[576,512]{1,0:T(8,128)} async-done(((f32[4608,512]{1,0:T(8,128)}), f32[576,512]{1,0:T(8,128)}) %reduce-scatter.24.cloned.1.call-update) | async-done | bytes 1179664 | tf_op jit(solution)/shard_map/reduce_scatter | solution.py:281
  772.2 8.5 add_convert_fusion
  780.7 30.6 %all-reduce.11.cloned.1.call-done = bf16[512,80]{0,1:T(8,128)(2,1)} async-done(((bf16[512,80]{0,1:T(8,128)(2,1)}), bf16[512,80]{0,1:T(8,128)(2,1)}) %all-reduce.11.cloned.1.call-update) | async-done | bytes 81936
  812.6 26.3 %reduce-scatter.48.cloned.1.call-done = bf16[128,256]{1,0:T(8,128)(2,1)} async-done(((bf16[512,256]{1,0:T(8,128)(2,1)}), bf16[128,256]{1,0:T(8,128)(2,1)}) %reduce-scatter.48.cloned.1.call-update) | async-done | bytes 65552
  840.5 25.1 %reduce-scatter.42.cloned.1.call-done = bf16[64,512]{1,0:T(8,128)(2,1)} async-done(((bf16[64,2048]{1,0:T(8,128)(2,1)}), bf16[64,512]{1,0:T(8,128)(2,1)}) %reduce-scatter.42.cloned.1.call-update) | async-done | bytes 65552 | tf_op jit(solution)/shard_map/reduce_scatter | solution.py:308
  867.2 25.6 %reduce-scatter.34.cloned.1.call-done = bf16[256,128]{0,1:T(8,128)(2,1)} async-done(((bf16[256,512]{0,1:T(8,128)(2,1)}), bf16[256,128]{0,1:T(8,128)(2,1)}) %reduce-scatter.34.cloned.1.call-update) | async-done | bytes 65552 | tf_op jit(solution)/shard_map/reduce_scatter | solution.py:302
  894.4 25.1 %reduce-scatter.38.cloned.1.call-done = bf16[256,128]{0,1:T(8,128)(2,1)} async-done(((bf16[256,512]{0,1:T(8,128)(2,1)}), bf16[256,128]{0,1:T(8,128)(2,1)}) %reduce-scatter.38.cloned.1.call-update) | async-done | bytes 65552 | tf_op jit(solution)/shard_map/reduce_scatter | solution.py:305
  921.1 25.5 %reduce-scatter.28.cloned.1.call-done = bf16[64,512]{1,0:T(8,128)(2,1)} async-done(((bf16[64,2048]{1,0:T(8,128)(2,1)}), bf16[64,512]{1,0:T(8,128)(2,1)}) %reduce-scatter.28.cloned.1.call-update) | async-done | bytes 65552 | tf_op jit(solution)/shard_map/reduce_scatter | solution.py:296
  948.1 26.0 %reduce-scatter.22.cloned.1.call-done = bf16[256,128]{0,1:T(8,128)(2,1)} async-done(((bf16[256,512]{0,1:T(8,128)(2,1)}), bf16[256,128]{0,1:T(8,128)(2,1)}) %reduce-scatter.22.cloned.1.call-update) | async-done | bytes 65552 | tf_op jit(solution)/shard_map/reduce_scatter | solution.py:290
  975.6 27.0 %reduce-scatter.46.cloned.1.call-done = bf16[128,576]{1,0:T(8,128)(2,1)} async-done(((bf16[512,576]{1,0:T(8,128)(2,1)}), bf16[128,576]{1,0:T(8,128)(2,1)}) %reduce-scatter.46.cloned.1.call-update) | async-done | bytes 147472
  (428 shorter events, 154.2 us)
Async XLA Ops:
  7.2 266.4 %copy-start = (bf16[10,2048]{1,0:T(8,128)(2,1)S(1)}, bf16[10,2048]{1,0:T(8,128)(2,1)}, u32[]{:S(2)}) copy-start(bf16[10,2048]{1,0:T(8,128)(2,1)} %param.45) | copy-start | bytes 122884
  7.2 34.4 %all-gather.10.cloned.1.call-start = ((), (), s32[]{:S(2)}) async-start(), calls=%async_computation.19 | async-start | bytes 2359296 | tf_op jit(solution)/shard_map/all_gather | solution.py:113
  7.9 149.2 %all-gather.12.cloned.1.call-start = ((), (), s32[]{:S(2)}) async-start(), calls=%async_computation.20 | async-start | bytes 5308416 | tf_op jit(solution)/shard_map/all_gather | solution.py:114
  8.7 200.1 %all-gather.14.cloned.1.call-start = ((), (), s32[]{:S(2)}) async-start(), calls=%async_computation.21 | async-start | bytes 2359296 | tf_op jit(solution)/shard_map/all_gather | solution.py:115
  9.4 264.1 %all-gather.18.cloned.1.call-start = ((), (), s32[]{:S(2)}) async-start(), calls=%async_computation.23 | async-start | bytes 2359296 | tf_op jit(solution)/shard_map/all_gather | solution.py:117
  10.0 280.9 %all-gather.20.cloned.1.call-start = ((), (), s32[]{:S(2)}) async-start(), calls=%async_computation.24 | async-start | bytes 2359296 | tf_op jit(solution)/shard_map/all_gather | solution.py:118
  10.6 298.0 %all-gather.16.cloned.1.call-start = ((), (), s32[]{:S(2)}) async-start(), calls=%async_computation.22 | async-start | bytes 2359296 | tf_op jit(solution)/shard_map/all_gather | solution.py:116
  11.2 126.1 %all-to-all-start = ((s32[8,1,8]{2,1,0:T(1,128)}), s32[8,1,8]{2,1,0:T(1,128)S(1)}, u32[]{:S(2)}, u32[]{:S(2)}) async-start(s32[8,1,8]{2,1,0:T(1,128)} %bitcast.138), calls=%async_computation | async-start | bytes 8192 | tf_op jit(solution)/shard_map/all_to_all | solution.py:171
  17.5 293.9 %all-gather.22.cloned.1.call-start = ((), (), s32[]{:S(2)}) async-start(), calls=%async_computation.25 | async-start | bytes 2359296 | tf_op jit(solution)/shard_map/all_gather | solution.py:119
  89.8 48.7 %collective-permute-start = (bf16[64,1,16,512]{3,2,0,1:T(8,128)(2,1)S(1)}, bf16[64,1,16,512]{3,2,0,1:T(8,128)(2,1)}, u32[]{:S(2)}, u32[]{:S(2)}) collective-permute-start(bf16[64,1,16,512]{3,2,0,1:T(8,128)(2,1)S(1)} %bitcast.117), channel_id=1, source_target_pairs={{0,1},{1,2},{2,3},{3,4},{4,5},{5,6},{6,7},{8,9},{9,10},{10,11},{11... | collective-permute-start | bytes 3145736 | tf_op jit(solution)/shard_map/ppermute | solution.py:15
  92.5 46.0 %collective-permute-start.1 = (bf16[64,1,16,512]{3,2,0,1:T(8,128)(2,1)S(1)}, bf16[64,1,16,512]{3,2,0,1:T(8,128)(2,1)}, u32[]{:S(2)}, u32[]{:S(2)}) collective-permute-start(bf16[64,1,16,512]{3,2,0,1:T(8,128)(2,1)S(1)} %bitcast.118), channel_id=1, source_target_pairs={{1,0},{2,1},{3,2},{4,3},{5,4},{6,5},{7,6},{9,8},{10,9},{11,10},{12... | collective-permute-start | bytes 3145736 | tf_op jit(solution)/shard_map/ppermute | solution.py:17
  270.1 37.2 %all-to-all-start.1 = ((bf16[8,8,2048]{2,1,0:T(8,128)(2,1)}), bf16[8,8,2048]{2,1,0:T(8,128)(2,1)S(1)}, u32[]{:S(2)}, u32[]{:S(2)}) async-start(bf16[8,8,2048]{2,1,0:T(8,128)(2,1)} %fusion.6), calls=%async_computation.1 | async-start | bytes 524288 | tf_op jit(solution)/shard_map/all_to_all | solution.py:170
  273.5 324.3 %reduce-scatter.44.cloned.1.call-start = ((), (), s32[]{:S(2)}) async-start(), calls=%async_computation.38 | async-start | bytes 1474560 | tf_op jit(solution)/shard_map/reduce_scatter | solution.py:287
  318.1 281.4 %reduce-scatter.30.cloned.1.call-start = ((), (), s32[]{:S(2)}) async-start(), calls=%async_computation.31 | async-start | bytes 4718592 | tf_op jit(solution)/shard_map/reduce_scatter | solution.py:283
  327.5 274.0 %reduce-scatter.40.cloned.1.call-start = ((), (), s32[]{:S(2)}) async-start(), calls=%async_computation.36 | async-start | bytes 4718592 | tf_op jit(solution)/shard_map/reduce_scatter | solution.py:286
  331.8 271.6 %reduce-scatter.32.cloned.1.call-start = ((), (), s32[]{:S(2)}) async-start(), calls=%async_computation.32 | async-start | bytes 4718592 | tf_op jit(solution)/shard_map/reduce_scatter | solution.py:284
  351.4 254.0 %reduce-scatter.36.cloned.1.call-start = ((), (), s32[]{:S(2)}) async-start(), calls=%async_computation.34 | async-start | bytes 4718592 | tf_op jit(solution)/shard_map/reduce_scatter | solution.py:285
  354.5 263.1 %reduce-scatter.26.cloned.1.call-start = ((), (), s32[]{:S(2)}) async-start(), calls=%async_computation.29 | async-start | bytes 4718592 | tf_op jit(solution)/shard_map/reduce_scatter | solution.py:282
  443.7 224.8 %reduce-scatter.20.cloned.1.call-start = ((), (), s32[]{:S(2)}) async-start(), calls=%async_computation.26 | async-start | bytes 4718592 | tf_op jit(solution)/shard_map/reduce_scatter | solution.py:280
  497.7 10.7 %collective-permute-start.2 = (bf16[64,1,16,512]{3,2,0,1:T(8,128)(2,1)S(1)}, bf16[64,1,16,512]{3,2,0,1:T(8,128)(2,1)}, u32[]{:S(2)}, u32[]{:S(2)}) collective-permute-start(bf16[64,1,16,512]{3,2,0,1:T(8,128)(2,1)S(1)} %bitcast.106), channel_id=1, source_target_pairs={{0,1},{1,2},{2,3},{3,4},{4,5},{5,6},{6,7},{8,9},{9,10},{10,11},{11... | collective-permute-start | bytes 3145736 | tf_op jit(solution)/shard_map/ppermute | solution.py:15
  500.4 8.0 collective-permute-start.3
  586.3 182.1 %reduce-scatter.24.cloned.1.call-start = ((), (), s32[]{:S(2)}) async-start(), calls=%async_computation.28 | async-start | bytes 10616832 | tf_op jit(solution)/shard_map/reduce_scatter | solution.py:281
  597.8 213.5 %all-reduce.11.cloned.1.call-start = ((), (), s32[]{:S(2)}) async-start(), calls=%async_computation.41 | async-start | bytes 163840
  599.4 239.5 %reduce-scatter.48.cloned.1.call-start = ((), (), s32[]{:S(2)}) async-start(), calls=%async_computation.40 | async-start | bytes 327680
  601.4 264.2 %reduce-scatter.42.cloned.1.call-start = ((), (), s32[]{:S(2)}) async-start(), calls=%async_computation.37 | async-start | bytes 327680 | tf_op jit(solution)/shard_map/reduce_scatter | solution.py:308
  603.3 168.8 %copy-start.5 = (bf16[1024,512]{1,0:T(8,128)(2,1)S(1)}, bf16[1024,512]{1,0:T(8,128)(2,1)}, u32[]{:S(2)}) copy-start(bf16[1024,512]{1,0:T(8,128)(2,1)} %copy-done.4) | copy-start | bytes 3145732
  603.3 289.4 %reduce-scatter.34.cloned.1.call-start = ((), (), s32[]{:S(2)}) async-start(), calls=%async_computation.33 | async-start | bytes 327680 | tf_op jit(solution)/shard_map/reduce_scatter | solution.py:302
  605.3 314.1 %reduce-scatter.38.cloned.1.call-start = ((), (), s32[]{:S(2)}) async-start(), calls=%async_computation.35 | async-start | bytes 327680 | tf_op jit(solution)/shard_map/reduce_scatter | solution.py:305
  607.2 339.4 %reduce-scatter.28.cloned.1.call-start = ((), (), s32[]{:S(2)}) async-start(), calls=%async_computation.30 | async-start | bytes 327680 | tf_op jit(solution)/shard_map/reduce_scatter | solution.py:296
  619.4 354.6 %reduce-scatter.22.cloned.1.call-start = ((), (), s32[]{:S(2)}) async-start(), calls=%async_computation.27 | async-start | bytes 327680 | tf_op jit(solution)/shard_map/reduce_scatter | solution.py:290
  670.3 332.3 %reduce-scatter.46.cloned.1.call-start = ((), (), s32[]{:S(2)}) async-start(), calls=%async_computation.39 | async-start | bytes 819200
  772.1 232.3 %copy-start.1 = (bf16[10,2048]{1,0:T(8,128)(2,1)S(1)}, bf16[10,2048]{1,0:T(8,128)(2,1)}, u32[]{:S(2)}) copy-start(bf16[10,2048]{1,0:T(8,128)(2,1)} %param.45) | copy-start | bytes 122884
  (121 other events, 7727.2 us)
Sparse Core Ops, SparseCore 0:
  9.6 31.8 all-gather.9
  43.2 51.9 all-gather.11
  96.8 35.5 all-gather.13
  133.9 28.7 all-gather.17
  164.2 29.0 all-gather.19
  194.7 28.8 all-gather.15
  225.2 29.4 all-gather.21
  318.2 34.8 reduce-scatter.43
  355.4 53.8 reduce-scatter.29
  411.4 49.2 reduce-scatter.39
  463.0 51.3 reduce-scatter.31
  516.6 50.5 reduce-scatter.35
  569.4 48.1 reduce-scatter.25
  620.4 48.1 reduce-scatter.19
  670.7 97.6 reduce-scatter.23
  771.7 39.4 all-reduce.10
  814.1 24.8 reduce-scatter.47
  841.5 24.0 reduce-scatter.41
  868.6 24.0 reduce-scatter.33
  895.4 24.0 reduce-scatter.37
  922.4 24.0 reduce-scatter.27
  949.9 24.0 reduce-scatter.21
  977.2 25.3 reduce-scatter.45
where the time goes:
time: 1020 us; the launch traced here: 1010 us
  waiting for transfers between devices  395 us (39%)
  blocking collectives  364 us (36%)
  matrix products  128 us (13%)
  local copies, waits for them, and re-layouts  45.6 us (4%)
  other arithmetic  43.2 us (4%)
  starting transfers between devices  18.9 us (2%)
  between operations  17.1 us (2%)
    psum x3, blocking collectives, normalize(): lax.psum((jnp.sum(field, 0), jnp.sum(field * field, 0)), ('batch', 'rows'))  126 us
    reduce_scatter x1, waiting for transfers between devices, on_device(): lax.psum_scatter(grad_wb, 'rows', scatter_dimension=0, tiled=True)  98 us
    psum x2, blocking collectives, segment_totals(): lax.psum((jnp.sum(grad, 0), jnp.sum(grad * normed, 0)), ('batch', 'rows'))  96 us
    unnamed x26, waiting for transfers between devices  88.4 us
    dot_general x11, matrix products, tdot(): lax.dot_general(left, right, (((0,), (0,)), ((), ())), preferred_element_...  49.2 us
    reduce_scatter x1, waiting for transfers between devices, on_device(): lax.psum_scatter(grad_wa, 'rows', scatter_dimension=0, tiled=True)  49.1 us
    all_gather x1, blocking collectives, on_device(): lax.all_gather(w_head, 'rows', axis=0, tiled=True)  39.7 us
    psum x1, blocking collectives, on_device(): lax.psum((jnp.sum(d_pre, 0), jnp.sum(d_pre * hat_c, 0), grad_ln_gain, gra...  38.9 us
  transfers between devices with their start and end apart: 29, of which 12 were waited for; matrix products, arithmetic and copies ran while one was open for 20% of the time, Pallas kernels for 0%

commit v1 on v0

--- a/solution.py
+++ b/solution.py
@@ -2,6 +2,18 @@
 import jax.numpy as jnp
 from jax import lax
 from jax.sharding import PartitionSpec as P
+
+
+def collect(array, axis, dim):
+    ways, here, lap = (lax.axis_size(axis), lax.axis_index(axis), array.shape[dim])
+    line, have = (array, 1)
+    while have < ways:
+        line = jnp.concatenate(
+            [line, lax.ppermute(line, axis, [(d, (d - have) % ways) for d in range(ways)])],
+            axis=dim,
+        )
+        have = 2 * have
+    return jnp.roll(line, here * lap, axis=dim)
 
 
 def padded(cells, sides, width):
@@ -110,7 +122,7 @@
     cell_count = clip_dev * row_dev * col_count
     total_count = cell_count * owners * lax.axis_size("batch")
     w_a, w_b, w_c, w_q, w_k, w_v, w_o, w_h = (
-        lax.all_gather(w_reduce, "rows", axis=0, tiled=True),
+        collect(w_reduce, "rows", 0),
         lax.all_gather(w_spatial, "rows", axis=0, tiled=True),
         lax.all_gather(w_expand, "rows", axis=0, tiled=True),
         lax.all_gather(query_weight, "rows", axis=0, tiled=True),

time: 1020 us -> 1120 us (1.098)
  local copies, waits for them, and re-layouts: 45.6 us -> 95.2 us
  waiting for transfers between devices: 395 us -> 441 us
    ppermute x0 -> x3, waiting for transfers between devices: none -> 93.2 us  [collect(): lax.ppermute(line, axis, [(d, (d - have) % ways) for d in range(ways)])]
    all_gather x1 -> x0, waiting for transfers between devices: 21.7 us -> none  [on_device(): lax.all_gather(w_reduce, 'rows', axis=0, tiled=True)]
    concatenate x1 -> x9, local copies, waits for them, and re-layouts: 0.07 us -> 18.5 us  [on_device(): jnp.concatenate([halo_d[:, 2 - row_step:2 - row_step + row_dev, 2 - col_s...]
    concatenate x1 -> x9, local copies, waits for them, and re-layouts: 1.15 us -> 18.6 us  [on_device(): jnp.concatenate([halo_a[:, row_step:row_step + row_dev, col_step:col_step...]
    reduce_scatter x1, waiting for transfers between devices: 49.1 us -> 36.1 us  [on_device(): lax.psum_scatter(grad_wa, 'rows', scatter_dimension=0, tiled=True)]
    unnamed x273 -> x334, local copies, waits for them, and re-layouts: 28.3 us -> 33.3 us
    unnamed x26 -> x25, waiting for transfers between devices: 88.4 us -> 86.5 us
  transfers between devices with their start and end apart: 29 -> 31, of which waited for: 12 -> 13; matrix products, arithmetic and copies ran while one was open for 20% -> 23% of each run, Pallas kernels for 0% -> 0%
where the time goes in v1:
time: 1120 us; the launch traced here: 1110 us
  waiting for transfers between devices  441 us (39%)
  blocking collectives  361 us (32%)
  matrix products  129 us (12%)
  local copies, waits for them, and re-layouts  95.2 us (8%)
  other arithmetic  43.2 us (4%)
  starting transfers between devices  21.9 us (2%)
  between operations  17.7 us (2%)
    psum x3, blocking collectives, normalize(): lax.psum((jnp.sum(field, 0), jnp.sum(field * field, 0)), ('batch', 'rows'))  123 us
    reduce_scatter x1, waiting for transfers between devices, on_device(): lax.psum_scatter(grad_wb, 'rows', scatter_dimension=0, tiled=True)  98 us
    psum x2, blocking collectives, segment_totals(): lax.psum((jnp.sum(grad, 0), jnp.sum(grad * normed, 0)), ('batch', 'rows'))  94 us
    ppermute x3, waiting for transfers between devices, collect(): lax.ppermute(line, axis, [(d, (d - have) % ways) for d in range(ways)])  93.2 us
    unnamed x25, waiting for transfers between devices  86.5 us
    dot_general x11, matrix products, tdot(): lax.dot_general(left, right, (((0,), (0,)), ((), ())), preferred_element_...  52.6 us
    all_gather x1, blocking collectives, on_device(): lax.all_gather(w_head, 'rows', axis=0, tiled=True)  42.6 us
    psum x1, blocking collectives, on_device(): lax.psum((jnp.sum(d_pre, 0), jnp.sum(d_pre * hat_c, 0), grad_ln_gain, gra...  39.1 us
  transfers between devices with their start and end apart: 31, of which 13 were waited for; matrix products, arithmetic and copies ran while one was open for 23% of the time, Pallas kernels for 0%

profile of v1, /device:TPU:0, one launch (start us, length us, event | category | flops | bytes accessed | tf_op | source)
XLA Modules:
  0.0 1110.0 jit_solution(3203136915428644195)
XLA Ops:
  21.0 35.9 %collective-permute-done.1 = bf16[512,512]{1,0:T(8,128)(2,1)S(1)} collective-permute-done((bf16[512,512]{1,0:T(8,128)(2,1)S(1)}, bf16[512,512]{1,0:T(8,128)(2,1)S(1)}, u32[]{:S(2)}, u32[]{:S(2)}) %collective-permute-start.1) | collective-permute-done | bytes 524320 | tf_op jit(solution)/shard_map/ppermute | solution.py:12
  63.1 53.1 %collective-permute-done.2 = bf16[1024,512]{1,0:T(8,128)(2,1)S(1)} collective-permute-done((bf16[1024,512]{1,0:T(8,128)(2,1)S(1)}, bf16[1024,512]{1,0:T(8,128)(2,1)S(1)}, u32[]{:S(2)}, u32[]{:S(2)}) %collective-permute-start.2) | collective-permute-done | bytes 1048608 | tf_op jit(solution)/shard_map/ppermute | solution.py:12
  119.0 42.5 %all-reduce.8 = (f32[512]{0:T(512)S(1)}, f32[512]{0:T(512)S(1)}) all-reduce(f32[512]{0:T(512)S(1)} %get-tuple-element.106, f32[512]{0:T(512)S(1)} %get-tuple-element.105), channel_id=1, replica_groups=mesh['batch'=4,'rows'=8] {'batch','rows'}, use_global_device_ids=true, to_apply=%region_3.4 | all-reduce | flops 1024 | bytes 8192 | tf_op jit(solution)/shard_map/psum | solution.py:75
  171.5 42.6 %all_gather.35 = bf16[4096,80]{0,1:T(8,128)(2,1)} all-gather(bf16[512,80]{0,1:T(8,128)(2,1)S(1)} %copy-done.16), channel_id=1, replica_groups=mesh['batch'=4,'rows'=8] {'rows'}, dimensions={0}, use_global_device_ids=true | all-gather | bytes 737280 | tf_op jit(solution)/shard_map/all_gather | solution.py:132
  257.8 10.1 fusion.61
  270.8 38.9 %all-reduce.7 = (f32[512]{0:T(512)S(1)}, f32[512]{0:T(512)S(1)}) all-reduce(f32[512]{0:T(512)S(1)} %get-tuple-element.104, f32[512]{0:T(512)S(1)} %get-tuple-element.103), channel_id=1, replica_groups=mesh['batch'=4,'rows'=8] {'batch','rows'}, use_global_device_ids=true, to_apply=%region_7.8 | all-reduce | flops 1024 | bytes 8192 | tf_op jit(solution)/shard_map/psum | solution.py:75
  310.0 8.3 fusion.58
  318.3 41.4 %all-reduce.6 = (f32[2048]{0:T(1024)S(1)}, f32[2048]{0:T(1024)S(1)}) all-reduce(f32[2048]{0:T(1024)S(1)} %get-tuple-element.98, f32[2048]{0:T(1024)S(1)} %get-tuple-element.97), channel_id=1, replica_groups=mesh['batch'=4,'rows'=8] {'batch','rows'}, use_global_device_ids=true, to_apply=%region_11.12 | all-reduce | flops 4096 | bytes 32768 | tf_op jit(solution)/shard_map/psum | solution.py:75
  360.3 10.1 fusion.6
  375.9 15.3 %all-gather = bf16[8,10,512]{2,1,0:T(8,128)(2,1)S(1)} all-gather(bf16[1,10,512]{2,1,0:T(8,128)(2,1)S(1)} %fusion.23), channel_id=1, replica_groups=mesh['batch'=4,'rows'=8] {'rows'}, dimensions={0}, use_global_device_ids=true | all-gather | bytes 92160 | tf_op jit(solution)/shard_map/all_gather | solution.py:195
  393.3 14.2 %all-gather.1 = bf16[8,10,512]{2,1,0:T(8,128)(2,1)S(1)} all-gather(bf16[1,10,512]{2,1,0:T(8,128)(2,1)S(1)} %fusion.24), channel_id=1, replica_groups=mesh['batch'=4,'rows'=8] {'rows'}, dimensions={0}, use_global_device_ids=true | all-gather | bytes 92160 | tf_op jit(solution)/shard_map/all_gather | solution.py:196
  432.4 16.0 %all_to_all.24 = bf16[8,10,1024]{2,1,0:T(8,128)(2,1)S(1)} all-to-all(bf16[8,10,1024]{2,1,0:T(8,128)(2,1)S(1)} %reshape.231), channel_id=1, replica_groups=mesh['batch'=4,'rows'=8] {'rows'}, dimensions={0} | all-to-all | bytes 327680 | tf_op jit(solution)/shard_map/all_to_all | solution.py:44
  458.3 17.6 %all_to_all.25 = bf16[8,8,2048]{2,1,0:T(8,128)(2,1)S(1)} all-to-all(bf16[8,8,2048]{2,1,0:T(8,128)(2,1)S(1)} %bitcast_select_fusion), channel_id=1, replica_groups=mesh['batch'=4,'rows'=8] {'rows'}, dimensions={0} | all-to-all | bytes 524288 | tf_op jit(solution)/shard_map/all_to_all | solution.py:254
  476.4 14.8 %fusion.57 = (f32[2048]{0:T(1024)S(1)}, f32[2048]{0:T(1024)S(1)}, f32[1024,2048]{1,0:T(8,128)}) fusion(f32[2048]{0:T(1024)S(1)} %get-tuple-element.197, f32[1024,2048]{1,0:T(8,128)} %get-tuple-element.207, f32[2048]{0:T(1024)S(1)} %get-tuple-element.198, bf16[1024,2048]{1,0:T(8,128)(2,1)} %bitcast.154, f32[2048]{0:T(1024)} %param.41, ...), kind=kOutput, calls=%fused_computation.256 | convolution fusion | flops 309587968 | bytes 21297152 | tf_op jit(solution)/shard_map/dot_general | solution.py:58
  491.2 39.1 %all-reduce.5 = (f32[2048]{0:T(1024)S(1)}, f32[2048]{0:T(1024)S(1)}) all-reduce(f32[2048]{0:T(1024)S(1)} %get-tuple-element.96, f32[2048]{0:T(1024)S(1)} %get-tuple-element.95), channel_id=1, replica_groups=mesh['batch'=4,'rows'=8] {'batch','rows'}, use_global_device_ids=true, to_apply=%region_22.23 | all-reduce | flops 4096 | bytes 32768 | tf_op jit(solution)/shard_map/psum | solution.py:257
  530.3 7.4 multiply_convert_fusion
  544.8 7.8 fusion.60
  552.5 42.7 %all-reduce.4 = (f32[512]{0:T(512)S(1)}, f32[512]{0:T(512)S(1)}) all-reduce(f32[512]{0:T(512)S(1)} %get-tuple-element.102, f32[512]{0:T(512)S(1)} %get-tuple-element.101), channel_id=1, replica_groups=mesh['batch'=4,'rows'=8] {'batch','rows'}, use_global_device_ids=true, to_apply=%region_26.27 | all-reduce | flops 1024 | bytes 8192 | tf_op jit(solution)/shard_map/psum | solution.py:82
  649.5 51.3 %all-reduce.3 = (f32[512]{0:T(512)S(1)}, f32[512]{0:T(512)S(1)}, f32[512]{0:T(512)}, f32[512]{0:T(512)}, f32[80]{0:T(128)}) all-reduce(f32[512]{0:T(512)S(1)} %get-tuple-element.100, f32[512]{0:T(512)S(1)} %get-tuple-element.99, f32[512]{0:T(512)S(1)} %copy-done.36, ...), channel_id=1, replica_groups=mesh['batch'=4,'rows'=8] {'batch','rows'}, use_global_device_ids=true, to_apply=%region_30.31 | all-reduce | flops 2128 | bytes 17024 | tf_op jit(solution)/shard_map/psum | solution.py:82
  700.8 7.6 convolution_bitcast_fusion.2
  708.5 11.4 %fusion.70 = f32[4608,512]{1,0:T(8,128)} fusion(bf16[1024,4608]{0,1:T(8,128)(2,1)} %constant_dynamic-update-slice_fusion.8, bf16[1024,512]{0,1:T(8,128)(2,1)S(1)} %multiply_convert_fusion.7), kind=kOutput, calls=%fused_computation.268 | convolution fusion | flops 4831838208 | bytes 19922944 | tf_op jit(solution)/shard_map/dot_general | solution.py:58
  731.1 36.1 %reduce-scatter.20.cloned.1.call-done = f32[256,512]{0,1:T(8,128)} async-done(((f32[2048,512]{0,1:T(8,128)}), f32[256,512]{0,1:T(8,128)}) %reduce-scatter.20.cloned.1.call-update) | async-done | bytes 524304 | tf_op jit(solution)/shard_map/reduce_scatter | solution.py:292
  769.1 98.0 %reduce-scatter.24.cloned.1.call-done = f32[576,512]{1,0:T(8,128)} async-done(((f32[4608,512]{1,0:T(8,128)}), f32[576,512]{1,0:T(8,128)}) %reduce-scatter.24.cloned.1.call-update) | async-done | bytes 1179664 | tf_op jit(solution)/shard_map/reduce_scatter | solution.py:293
  870.9 9.7 add_convert_fusion
  880.6 29.3 %all-reduce.11.cloned.1.call-done = bf16[512,80]{0,1:T(8,128)(2,1)} async-done(((bf16[512,80]{0,1:T(8,128)(2,1)}), bf16[512,80]{0,1:T(8,128)(2,1)}) %all-reduce.11.cloned.1.call-update) | async-done | bytes 81936
  911.3 26.3 %reduce-scatter.48.cloned.1.call-done = bf16[128,256]{1,0:T(8,128)(2,1)} async-done(((bf16[512,256]{1,0:T(8,128)(2,1)}), bf16[128,256]{1,0:T(8,128)(2,1)}) %reduce-scatter.48.cloned.1.call-update) | async-done | bytes 65552
  939.2 25.1 %reduce-scatter.42.cloned.1.call-done = bf16[64,512]{1,0:T(8,128)(2,1)} async-done(((bf16[64,2048]{1,0:T(8,128)(2,1)}), bf16[64,512]{1,0:T(8,128)(2,1)}) %reduce-scatter.42.cloned.1.call-update) | async-done | bytes 65552 | tf_op jit(solution)/shard_map/reduce_scatter | solution.py:320
  965.8 25.5 %reduce-scatter.34.cloned.1.call-done = bf16[256,128]{0,1:T(8,128)(2,1)} async-done(((bf16[256,512]{0,1:T(8,128)(2,1)}), bf16[256,128]{0,1:T(8,128)(2,1)}) %reduce-scatter.34.cloned.1.call-update) | async-done | bytes 65552 | tf_op jit(solution)/shard_map/reduce_scatter | solution.py:314
  992.9 25.3 %reduce-scatter.38.cloned.1.call-done = bf16[256,128]{0,1:T(8,128)(2,1)} async-done(((bf16[256,512]{0,1:T(8,128)(2,1)}), bf16[256,128]{0,1:T(8,128)(2,1)}) %reduce-scatter.38.cloned.1.call-update) | async-done | bytes 65552 | tf_op jit(solution)/shard_map/reduce_scatter | solution.py:317
  1019.8 25.4 %reduce-scatter.28.cloned.1.call-done = bf16[64,512]{1,0:T(8,128)(2,1)} async-done(((bf16[64,2048]{1,0:T(8,128)(2,1)}), bf16[64,512]{1,0:T(8,128)(2,1)}) %reduce-scatter.28.cloned.1.call-update) | async-done | bytes 65552 | tf_op jit(solution)/shard_map/reduce_scatter | solution.py:308
  1046.6 25.9 %reduce-scatter.22.cloned.1.call-done = bf16[256,128]{0,1:T(8,128)(2,1)} async-done(((bf16[256,512]{0,1:T(8,128)(2,1)}), bf16[256,128]{0,1:T(8,128)(2,1)}) %reduce-scatter.22.cloned.1.call-update) | async-done | bytes 65552 | tf_op jit(solution)/shard_map/reduce_scatter | solution.py:302
  1074.2 27.0 %reduce-scatter.46.cloned.1.call-done = bf16[128,576]{1,0:T(8,128)(2,1)} async-done(((bf16[512,576]{1,0:T(8,128)(2,1)}), bf16[128,576]{1,0:T(8,128)(2,1)}) %reduce-scatter.46.cloned.1.call-update) | async-done | bytes 147472
  (513 shorter events, 210.7 us)
Async XLA Ops:
  7.2 366.8 %copy-start = (bf16[10,2048]{1,0:T(8,128)(2,1)S(1)}, bf16[10,2048]{1,0:T(8,128)(2,1)}, u32[]{:S(2)}) copy-start(bf16[10,2048]{1,0:T(8,128)(2,1)} %param.45) | copy-start | bytes 122884
  7.2 250.5 %all-gather.9.cloned.1.call-start = ((), (), s32[]{:S(2)}) async-start(), calls=%async_computation.19 | async-start | bytes 5308416 | tf_op jit(solution)/shard_map/all_gather | solution.py:126
  8.0 301.8 %all-gather.11.cloned.1.call-start = ((), (), s32[]{:S(2)}) async-start(), calls=%async_computation.20 | async-start | bytes 2359296 | tf_op jit(solution)/shard_map/all_gather | solution.py:127
  8.7 365.2 %all-gather.15.cloned.1.call-start = ((), (), s32[]{:S(2)}) async-start(), calls=%async_computation.22 | async-start | bytes 2359296 | tf_op jit(solution)/shard_map/all_gather | solution.py:129
  9.5 381.9 %all-gather.17.cloned.1.call-start = ((), (), s32[]{:S(2)}) async-start(), calls=%async_computation.23 | async-start | bytes 2359296 | tf_op jit(solution)/shard_map/all_gather | solution.py:130
  10.0 398.8 %all-gather.13.cloned.1.call-start = ((), (), s32[]{:S(2)}) async-start(), calls=%async_computation.21 | async-start | bytes 2359296 | tf_op jit(solution)/shard_map/all_gather | solution.py:128
  10.6 8.7 collective-permute-start
  20.4 36.5 %collective-permute-start.1 = (bf16[512,512]{1,0:T(8,128)(2,1)S(1)}, bf16[512,512]{1,0:T(8,128)(2,1)S(1)}, u32[]{:S(2)}, u32[]{:S(2)}) collective-permute-start(bf16[512,512]{1,0:T(8,128)(2,1)S(1)} %pad_maximum_fusion.4), channel_id=1, source_target_pairs={{0,6},{1,7},{2,0},{3,1},{4,2},{5,3},{6,4},{7,5},{8,14},{9,15},{10,... | collective-permute-start | bytes 1572872 | tf_op jit(solution)/shard_map/ppermute | solution.py:12
  57.9 58.3 %collective-permute-start.2 = (bf16[1024,512]{1,0:T(8,128)(2,1)S(1)}, bf16[1024,512]{1,0:T(8,128)(2,1)S(1)}, u32[]{:S(2)}, u32[]{:S(2)}) collective-permute-start(bf16[1024,512]{1,0:T(8,128)(2,1)S(1)} %pad_maximum_fusion), channel_id=1, source_target_pairs={{0,4},{1,5},{2,6},{3,7},{4,0},{5,1},{6,2},{7,3},{8,12},{9,13},{10,... | collective-permute-start | bytes 3145736 | tf_op jit(solution)/shard_map/ppermute | solution.py:12
  57.9 156.6 %all-to-all-start = ((s32[8,1,8]{2,1,0:T(1,128)}), s32[8,1,8]{2,1,0:T(1,128)S(1)}, u32[]{:S(2)}, u32[]{:S(2)}) async-start(s32[8,1,8]{2,1,0:T(1,128)} %bitcast.1), calls=%async_computation | async-start | bytes 8192 | tf_op jit(solution)/shard_map/all_to_all | solution.py:183
  62.1 349.5 %all-gather.19.cloned.1.call-start = ((), (), s32[]{:S(2)}) async-start(), calls=%async_computation.24 | async-start | bytes 2359296 | tf_op jit(solution)/shard_map/all_gather | solution.py:131
  164.3 51.6 %collective-permute-start.3 = (bf16[64,1,16,512]{3,2,0,1:T(8,128)(2,1)}, bf16[64,1,16,512]{3,2,0,1:T(8,128)(2,1)}, u32[]{:S(2)}, u32[]{:S(2)}) collective-permute-start(bf16[64,1,16,512]{3,2,0,1:T(8,128)(2,1)} %bitcast.4), channel_id=1, source_target_pairs={{0,1},{1,2},{2,3},{3,4},{4,5},{5,6},{6,7},{8,9},{9,10},{10,11},{11... | collective-permute-start | bytes 3145736 | tf_op jit(solution)/shard_map/ppermute | solution.py:27
  167.0 48.8 %collective-permute-start.4 = (bf16[64,1,16,512]{3,2,0,1:T(8,128)(2,1)}, bf16[64,1,16,512]{3,2,0,1:T(8,128)(2,1)S(1)}, u32[]{:S(2)}, u32[]{:S(2)}) collective-permute-start(bf16[64,1,16,512]{3,2,0,1:T(8,128)(2,1)} %bitcast.4), channel_id=1, source_target_pairs={{1,0},{2,1},{3,2},{4,3},{5,4},{6,5},{7,6},{9,8},{10,9},{11,10},{12... | collective-permute-start | bytes 3145736 | tf_op jit(solution)/shard_map/ppermute | solution.py:29
  370.5 37.1 %all-to-all-start.1 = ((bf16[8,8,2048]{2,1,0:T(8,128)(2,1)}), bf16[8,8,2048]{2,1,0:T(8,128)(2,1)S(1)}, u32[]{:S(2)}, u32[]{:S(2)}) async-start(bf16[8,8,2048]{2,1,0:T(8,128)(2,1)} %fusion.6), calls=%async_computation.1 | async-start | bytes 524288 | tf_op jit(solution)/shard_map/all_to_all | solution.py:182
  373.9 346.0 %reduce-scatter.44.cloned.1.call-start = ((), (), s32[]{:S(2)}) async-start(), calls=%async_computation.37 | async-start | bytes 1474560 | tf_op jit(solution)/shard_map/reduce_scatter | solution.py:299
  418.3 303.3 %reduce-scatter.30.cloned.1.call-start = ((), (), s32[]{:S(2)}) async-start(), calls=%async_computation.30 | async-start | bytes 4718592 | tf_op jit(solution)/shard_map/reduce_scatter | solution.py:295
  427.8 295.8 %reduce-scatter.40.cloned.1.call-start = ((), (), s32[]{:S(2)}) async-start(), calls=%async_computation.35 | async-start | bytes 4718592 | tf_op jit(solution)/shard_map/reduce_scatter | solution.py:298
  431.9 293.6 %reduce-scatter.32.cloned.1.call-start = ((), (), s32[]{:S(2)}) async-start(), calls=%async_computation.31 | async-start | bytes 4718592 | tf_op jit(solution)/shard_map/reduce_scatter | solution.py:296
  451.2 276.2 %reduce-scatter.36.cloned.1.call-start = ((), (), s32[]{:S(2)}) async-start(), calls=%async_computation.33 | async-start | bytes 4718592 | tf_op jit(solution)/shard_map/reduce_scatter | solution.py:297
  454.3 274.9 %reduce-scatter.26.cloned.1.call-start = ((), (), s32[]{:S(2)}) async-start(), calls=%async_computation.28 | async-start | bytes 4718592 | tf_op jit(solution)/shard_map/reduce_scatter | solution.py:294
  544.7 222.5 %reduce-scatter.20.cloned.1.call-start = ((), (), s32[]{:S(2)}) async-start(), calls=%async_computation.25 | async-start | bytes 4718592 | tf_op jit(solution)/shard_map/reduce_scatter | solution.py:292
  599.4 10.8 collective-permute-start.5
  602.1 8.1 collective-permute-start.6
  708.4 158.7 %reduce-scatter.24.cloned.1.call-start = ((), (), s32[]{:S(2)}) async-start(), calls=%async_computation.27 | async-start | bytes 10616832 | tf_op jit(solution)/shard_map/reduce_scatter | solution.py:293
  719.8 190.1 %all-reduce.11.cloned.1.call-start = ((), (), s32[]{:S(2)}) async-start(), calls=%async_computation.40 | async-start | bytes 163840
  721.5 216.1 %reduce-scatter.48.cloned.1.call-start = ((), (), s32[]{:S(2)}) async-start(), calls=%async_computation.39 | async-start | bytes 327680
  723.5 240.8 %reduce-scatter.42.cloned.1.call-start = ((), (), s32[]{:S(2)}) async-start(), calls=%async_computation.36 | async-start | bytes 327680 | tf_op jit(solution)/shard_map/reduce_scatter | solution.py:320
  725.4 265.9 %reduce-scatter.34.cloned.1.call-start = ((), (), s32[]{:S(2)}) async-start(), calls=%async_computation.32 | async-start | bytes 327680 | tf_op jit(solution)/shard_map/reduce_scatter | solution.py:314
  727.3 290.9 %reduce-scatter.38.cloned.1.call-start = ((), (), s32[]{:S(2)}) async-start(), calls=%async_computation.34 | async-start | bytes 327680 | tf_op jit(solution)/shard_map/reduce_scatter | solution.py:317
  729.2 315.9 %reduce-scatter.28.cloned.1.call-start = ((), (), s32[]{:S(2)}) async-start(), calls=%async_computation.29 | async-start | bytes 327680 | tf_op jit(solution)/shard_map/reduce_scatter | solution.py:308
  731.1 341.5 %reduce-scatter.22.cloned.1.call-start = ((), (), s32[]{:S(2)}) async-start(), calls=%async_computation.26 | async-start | bytes 327680 | tf_op jit(solution)/shard_map/reduce_scatter | solution.py:302
  769.0 332.1 %reduce-scatter.46.cloned.1.call-start = ((), (), s32[]{:S(2)}) async-start(), calls=%async_computation.38 | async-start | bytes 819200
  (150 other events, 9904.9 us)
Sparse Core Ops, SparseCore 0:
  9.7 92.7 all-gather.8
  104.1 31.4 all-gather.10
  137.2 29.0 all-gather.14
  167.8 35.2 all-gather.16
  204.6 30.8 all-gather.12
  236.9 28.5 all-gather.18
  418.4 34.9 reduce-scatter.43
  455.7 53.5 reduce-scatter.29
  511.5 49.1 reduce-scatter.39
  562.8 50.1 reduce-scatter.31
  615.4 49.3 reduce-scatter.35
  667.0 49.1 reduce-scatter.25
  719.1 48.1 reduce-scatter.19
  769.4 97.6 reduce-scatter.23
  870.4 39.4 all-reduce.10
  912.7 24.8 reduce-scatter.47
  940.2 24.0 reduce-scatter.41
  967.2 24.0 reduce-scatter.33
  994.1 24.0 reduce-scatter.37
  1021.0 24.0 reduce-scatter.27
  1048.5 24.0 reduce-scatter.21
  1075.7 25.3 reduce-scatter.45
